TPU v7x, 32 devices: a whole 2x2x4 slice. The times are simulated.
32 devices in a mesh: groups: 2 (over y), seq: 4 (over z), mp: 2 (over x), enc: 2 (over core).
Axes of the slice: x: 2, y: 2, z: 4, core: 2. Of those that a mesh axis runs over, the one named last changes fastest.
Arguments:
- tokens: bfloat16 [4096, 4096], P(('groups', 'seq'), ('mp', 'enc')), parts along dimension 0, may hold values from -6 to 6
- nbr_feats: bfloat16 [192, 128, 4096], P(('groups', 'seq'), None, ('mp', 'enc')), parts along dimension 0, may hold values from -6 to 6
- counts: int32 [8], P('groups'), parts along dimension 0, may hold values from 8 to 24, as said below
- slot_target: int32 [192], P(('groups', 'seq')), parts along dimension 0, may hold values from 0 to 63, as said below
- w_query: bfloat16 [4096, 512], P(None, ('mp', 'enc')), may hold values from -32 to 32
- w_keyval: bfloat16 [4096, 512], P(None, ('mp', 'enc')), may hold values from -1 to 1
Outputs:
- attended: bfloat16 [4096, 512], P(('groups', 'seq'), ('mp', 'enc')), parts along dimension 0
There are 2 independent parts, one for each index of `groups`. A program takes and returns all parts, laid end to end along the dimension named above; an argument that names none is the same for every part. Nothing has to cross between parts.
Inputs may be any that keep to these rules, and one draw needn't show every extreme that they name: Each seq index's live slots are its first counts slots; the counts sum to 64. `slot_target`: A live slot holds neighbour o * 16 + l of the spans of seq index o; every neighbour is held by exactly one live slot; the live slots of one seq index hold at most 8 neighbours of any one seq index; dead slots hold arbitrary values of the range.
All inputs are finite; a program needn't handle non-finite values.
Results may differ from a plain program's by a relative error of at most 0.003.
The roundings to bfloat16 on the way count: a program that leaves them out, or rounds other values in their place, can miss the bound.
Values may be sent and summed in bfloat16 or wider, within the bound.
A program may use at most 128 MiB of HBM per device.

v0:
```python
import jax
import jax.numpy as jnp
from jax import lax
from jax.sharding import PartitionSpec as P

D = 4096
SPAN = 64
NBR = 2
RLEN = 128
CH_SEQ = 8
NB_SEQ = 16
ENC_CAP = 24
epsilon = 1e-05


def partner_2(block, axis, stride):
    count = lax.axis_size(axis)
    route = []
    for low in range(count):
        high = low | 1 << stride
        if high != low and high < count:
            route += [(low, high), (high, low)]
    return lax.ppermute(block, axis, route)


def passed_along(block, axis, distance):
    devices = range(lax.axis_size(axis))
    route = [(i - distance, i) for i in devices if i - distance in devices]
    return lax.ppermute(block, axis, route)


def project_fold(weight, piece):
    width = piece.shape[-1]
    flat_rows = piece.reshape(-1, width)
    mine = lax.all_to_all(weight, ("mp", "enc"), split_axis=0, concat_axis=1, tiled=True)
    partial = jnp.dot(flat_rows, mine, preferred_element_type=jnp.float32)
    running = lax.psum_scatter(partial, ("mp", "enc"), scatter_dimension=1, tiled=True)
    widened = flat_rows.astype(jnp.float32)
    squares = lax.psum(jnp.sum(widened * widened, axis=1), ("mp", "enc"))
    return (running, squares)


def normalized(carry, factor):
    running, squares = carry
    scale_rows = lax.rsqrt(squares / D + epsilon) * factor
    return (running * scale_rows[:, None]).astype(jnp.bfloat16)


def routing_plan(slot_target, counts, pair_cap):
    seq_count = counts.shape[0]
    seq_here = lax.axis_index("seq")
    live_count = jnp.sum(jnp.where(jnp.arange(seq_count) == seq_here, counts, 0))
    slot_ids = jnp.arange(ENC_CAP)
    live_slots = slot_ids < live_count
    owner_of = slot_target // NB_SEQ
    position = slot_target % NB_SEQ
    same_owner = (
        (owner_of[:, None] == owner_of[None, :])
        & live_slots[None, :]
        & (slot_ids[None, :] < slot_ids[:, None])
    )
    rank_within = jnp.sum(same_owner.astype(jnp.int32), axis=1)
    target_slot = owner_of * pair_cap + rank_within
    buffer_ids = jnp.arange(seq_count * pair_cap)
    chosen = (buffer_ids[:, None] == target_slot[None, :]) & live_slots[None, :]
    sent_ids = jnp.sum(jnp.where(chosen, position[None, :] + 1, 0), axis=1) - 1
    return (chosen, sent_ids.reshape(seq_count, pair_cap))


def pack_rows(chosen, payload, seq_count, pair_cap):
    packed = jnp.dot(chosen.astype(jnp.bfloat16), payload, preferred_element_type=jnp.float32)
    return packed.astype(jnp.bfloat16).reshape(seq_count, pair_cap, payload.shape[1])


def place_rows(received, received_ids):
    flat_rows = received.reshape(-1, received.shape[-1])
    picker = received_ids.reshape(1, -1) == jnp.arange(NB_SEQ)[:, None]
    placed = jnp.dot(picker.astype(jnp.bfloat16), flat_rows, preferred_element_type=jnp.float32)
    return placed.astype(jnp.bfloat16)


def local(tokens, nbr_feats, counts, slot_target, w_query, w_keyval):
    seq_count = lax.axis_size("seq")
    pair_cap = max(2, 2 * NB_SEQ // seq_count)
    head_size = w_keyval.shape[1]
    chosen, sent_ids = routing_plan(slot_target, counts, pair_cap)
    folded = project_fold(w_keyval, nbr_feats)
    encoded = normalized(folded, 1.0).reshape(ENC_CAP, RLEN * head_size)
    packed = pack_rows(chosen, encoded, seq_count, pair_cap)
    received, received_ids = (
        lax.all_to_all(packed, "seq", split_axis=0, concat_axis=0, tiled=True),
        lax.all_to_all(sent_ids, "seq", split_axis=0, concat_axis=0, tiled=True),
    )
    own_half = place_rows(received, received_ids).reshape(NB_SEQ, RLEN, head_size)
    partner = partner_2(own_half, "enc", 0)
    first_lane = lax.axis_index("enc") == 0
    key_rows = jnp.where(first_lane, own_half, partner).reshape(CH_SEQ, NBR * RLEN, head_size)
    value_rows = jnp.where(first_lane, partner, own_half).reshape(CH_SEQ, NBR * RLEN, head_size)
    prior_keys, prior_values = passed_along((key_rows[-1], value_rows[-1]), "seq", 1)
    context_keys = jnp.concatenate([prior_keys[None], key_rows[:-1]], axis=0)
    context_values = jnp.concatenate([prior_values[None], value_rows[:-1]], axis=0)
    folded_tokens = project_fold(w_query, tokens)
    queries = normalized(folded_tokens, head_size ** (-0.5)).reshape(CH_SEQ, SPAN, head_size)
    scores = jnp.einsum("cqd,ckd->cqk", queries, context_keys, preferred_element_type=jnp.float32)
    weights = jax.nn.softmax(scores, axis=-1).astype(jnp.bfloat16)
    attended = jnp.einsum(
        "cqk,ckd->cqd", weights, context_values, preferred_element_type=jnp.float32
    )
    return attended.astype(jnp.bfloat16).reshape(CH_SEQ * SPAN, head_size)


def solution(mesh):
    placed = (
        P(("groups", "seq"), ("mp", "enc")),
        P(("groups", "seq"), None, ("mp", "enc")),
        P("groups"),
        P(("groups", "seq")),
        P(None, ("mp", "enc")),
        P(None, ("mp", "enc")),
    )
    return jax.shard_map(
        local,
        mesh=mesh,
        in_specs=placed,
        out_specs=P(("groups", "seq"), ("mp", "enc")),
        check_vma=False,
    )
```

profile of v0, /device:TPU:0, one launch (start us, length us, event | category | flops | bytes accessed | tf_op | source)
XLA Modules:
  0.0 157.2 jit_solution(10711013462824801652)
XLA Ops:
  6.5 18.7 %all_to_all.49 = bf16[4,1024,128]{2,1,0:T(8,128)(2,1)S(1)} all-to-all(bf16[4,1024,128]{2,1,0:T(8,128)(2,1)} %bitcast.41), channel_id=1, replica_groups=mesh['groups'=2,'seq'=4,'mp'=2,'enc'=2] {'mp','enc'}, dimensions={0} | all-to-all | bytes 2097152 | tf_op jit(solution)/shard_map/all_to_all | solution.py:35
  25.2 0.5 copy.14
  25.7 8.2 %fusion.33 = f32[3072,512]{1,0:T(8,128)} fusion(bf16[3072,1024]{1,0:T(8,128)(2,1)} %bitcast.35, bf16[1024,512]{0,1:T(8,128)(2,1)S(1)} %bitcast.42), kind=kOutput, calls=%fused_computation.53 | convolution fusion | flops 3221225472 | bytes 13631488 | tf_op jit(solution)/shard_map/dot_general | solution.py:36
  34.0 0.6 copy-done.1
  34.6 0.6 fusion.22
  35.3 0.6 iota_compare_fusion.4
  36.3 0.7 sub.20
  36.9 5.6 %all-to-all-start.1 = ((s32[4,1,8]{2,1,0:T(1,128)}), s32[4,1,8]{2,1,0:T(1,128)S(1)}, u32[]{:S(2)}, u32[]{:S(2)}) async-start(s32[4,1,8]{2,1,0:T(1,128)} %bitcast.4), calls=%async_computation.2 | async-start | bytes 4096 | tf_op jit(solution)/shard_map/all_to_all | solution.py:92
  42.8 5.6 %multiply_reduce_fusion = f32[24,128]{1,0:T(8,128)S(1)} fusion(bf16[24,128,1024]{2,1,0:T(8,128)(2,1)} %param.7), kind=kLoop, calls=%fused_computation.4 | loop fusion | flops 9434112 | bytes 6303744 | tf_op jit(solution)/shard_map/reduce_sum | solution.py:39
  48.4 10.1 %all-reduce = (f32[3072]{0:T(1024)S(1)}, f32[512]{0:T(512)S(1)}) all-reduce(f32[3072]{0:T(1024)S(1)} %bitcast.51, f32[512]{0:T(512)S(1)} %multiply_reduce_fusion.1), channel_id=1, replica_groups=mesh['groups'=2,'seq'=4,'mp'=2,'enc'=2] {'mp','enc'}, use_global_device_ids=true, to_apply=%region_8.9 | all-reduce | flops 3584 | bytes 28672 | tf_op jit(solution)/shard_map/psum | solution.py:39
  58.5 3.5 %all-to-all-start = ((bf16[4,1024,128]{2,1,0:T(8,128)(2,1)}), bf16[4,1024,128]{2,1,0:T(8,128)(2,1)S(1)}, u32[]{:S(2)}, u32[]{:S(2)}) async-start(bf16[4,1024,128]{2,1,0:T(8,128)(2,1)} %bitcast), calls=%async_computation | async-start | bytes 2097152 | tf_op jit(solution)/shard_map/all_to_all | solution.py:35
  62.1 42.8 %reduce-scatter.5.cloned.1.call-done = f32[3072,128]{1,0:T(8,128)} async-done(((f32[3072,512]{1,0:T(8,128)}), f32[3072,128]{1,0:T(8,128)}) %reduce-scatter.5.cloned.1.call-update) | async-done | bytes 1572880 | tf_op jit(solution)/shard_map/reduce_scatter | solution.py:37
  104.8 1.9 %multiply_convert_fusion = bf16[3072,128]{1,0:T(8,128)(2,1)S(1)} fusion(f32[3072,128]{1,0:T(8,128)} %reduce-scatter.5.cloned.1.call-done, f32[3072]{0:T(1024)S(1)} %add_rsqrt_fusion), kind=kLoop, calls=%fused_computation.6 | loop fusion | flops 786432 | bytes 2371584 | tf_op jit(solution)/shard_map/convert_element_type | solution.py:46
  107.1 1.5 fusion.1
  108.6 4.6 %all-to-all-start.3 = ((bf16[4,8,16384]{2,1,0:T(8,128)(2,1)}), bf16[4,8,16384]{2,1,0:T(8,128)(2,1)S(1)}, u32[]{:S(2)}, u32[]{:S(2)}) async-start(bf16[4,8,16384]{2,1,0:T(8,128)(2,1)} %fusion.1), calls=%async_computation.5 | async-start | bytes 2097152 | tf_op jit(solution)/shard_map/all_to_all | solution.py:91
  113.8 3.0 %fusion.32 = f32[512,512]{1,0:T(8,128)} fusion(bf16[512,1024]{1,0:T(8,128)(2,1)} %param.6, bf16[1024,512]{0,1:T(8,128)(2,1)S(1)} %bitcast.43), kind=kOutput, calls=%fused_computation.52 | convolution fusion | flops 536870912 | bytes 3145728 | tf_op jit(solution)/shard_map/dot_general | solution.py:36
  117.3 0.7 reduce.4
  118.1 20.9 %all-to-all-done.3 = bf16[4,8,16384]{2,1,0:T(8,128)(2,1)S(1)} async-done(((bf16[4,8,16384]{2,1,0:T(8,128)(2,1)}), bf16[4,8,16384]{2,1,0:T(8,128)(2,1)S(1)}, u32[]{:S(2)}, u32[]{:S(2)}) %all-to-all-start.3) | async-done | bytes 1048608 | tf_op jit(solution)/shard_map/all_to_all | solution.py:91
  139.4 1.9 %collective-permute-done = bf16[16,128,128]{2,1,0:T(8,128)(2,1)S(1)} collective-permute-done((bf16[16,128,128]{2,1,0:T(8,128)(2,1)S(1)}, bf16[16,128,128]{2,1,0:T(8,128)(2,1)S(1)}, u32[]{:S(2)}, u32[]{:S(2)}) %collective-permute-start) | collective-permute-done | bytes 524320 | tf_op jit(solution)/shard_map/ppermute | solution.py:23
  141.4 1.3 collective-permute-start.1
  142.8 1.1 multiply_convert_fusion.1
  143.9 2.9 %collective-permute-start.2 = (bf16[256,128]{1,0:T(8,128)(2,1)S(1)}, bf16[256,128]{1,0:T(8,128)(2,1)S(1)}, u32[]{:S(2)}, u32[]{:S(2)}) collective-permute-start(bf16[256,128]{1,0:T(8,128)(2,1)S(1)} %bitcast.50), channel_id=1, source_target_pairs={{0,4},{4,8},{8,12},{1,5},{5,9},{9,13},{2,6},{6,10},{10,14},{3,7},{... | collective-permute-start | bytes 196616 | tf_op jit(solution)/shard_map/ppermute | solution.py:29
  147.6 1.1 collective-permute-done.2
  148.7 1.6 %convolution_convert_fusion.2 = bf16[8,64,128]{2,1,0:T(8,128)(2,1)} fusion(bf16[7,256,128]{2,1,0:T(8,128)(2,1)S(1)} %bitcast.46, bf16[1,256,128]{2,1,0:T(8,128)(2,1)S(1)} %bitcast.52, f32[8,64]{1,0:T(8,128)S(1)} %fusion.29, f32[8,64,256]{2,1,0:T(8,128)S(1)} %fusion.6), kind=kOutput, calls=%fused_computation.10 | convolution fusion | flops 34276096 | bytes 1181696 | tf_op jit(solution)/shard_map/cqk,ckd->cqd/dot_general | solution.py:106
  (35 shorter events, 3.5 us)
Async XLA Ops:
  6.5 98.3 %reduce-scatter.5.cloned.1.call-start = ((), (), s32[]{:S(2)}) async-start(), calls=%async_computation.7 | async-start | bytes 7864320 | tf_op jit(solution)/shard_map/reduce_scatter | solution.py:37
  34.0 0.7 copy-start.1
  34.0 1.9 %copy-start.2 = (s32[24]{0:T(128)S(1)}, s32[24]{0:T(128)}, u32[]{:S(2)}) copy-start(s32[24]{0:T(128)} %param.9) | copy-start | bytes 292
  34.0 8.5 %copy-start = (bf16[512,1024]{1,0:T(8,128)(2,1)S(1)}, bf16[512,1024]{1,0:T(8,128)(2,1)}, u32[]{:S(2)}) copy-start(bf16[512,1024]{1,0:T(8,128)(2,1)} %param.6) | copy-start | bytes 3145732
  36.9 21.6 %all-to-all-start.1 = ((s32[4,1,8]{2,1,0:T(1,128)}), s32[4,1,8]{2,1,0:T(1,128)S(1)}, u32[]{:S(2)}, u32[]{:S(2)}) async-start(s32[4,1,8]{2,1,0:T(1,128)} %bitcast.4), calls=%async_computation.2 | async-start | bytes 4096 | tf_op jit(solution)/shard_map/all_to_all | solution.py:92
  58.5 50.1 %all-to-all-start = ((bf16[4,1024,128]{2,1,0:T(8,128)(2,1)}), bf16[4,1024,128]{2,1,0:T(8,128)(2,1)S(1)}, u32[]{:S(2)}, u32[]{:S(2)}) async-start(bf16[4,1024,128]{2,1,0:T(8,128)(2,1)} %bitcast), calls=%async_computation | async-start | bytes 2097152 | tf_op jit(solution)/shard_map/all_to_all | solution.py:35
  108.6 30.3 %all-to-all-start.3 = ((bf16[4,8,16384]{2,1,0:T(8,128)(2,1)}), bf16[4,8,16384]{2,1,0:T(8,128)(2,1)S(1)}, u32[]{:S(2)}, u32[]{:S(2)}) async-start(bf16[4,8,16384]{2,1,0:T(8,128)(2,1)} %fusion.1), calls=%async_computation.5 | async-start | bytes 2097152 | tf_op jit(solution)/shard_map/all_to_all | solution.py:91
  113.2 29.5 %reduce-scatter.3.cloned.1.call-start = ((), (), s32[]{:S(2)}) async-start(), calls=%async_computation.6 | async-start | bytes 1310720 | tf_op jit(solution)/shard_map/reduce_scatter | solution.py:37
  139.3 2.0 %collective-permute-start = (bf16[16,128,128]{2,1,0:T(8,128)(2,1)S(1)}, bf16[16,128,128]{2,1,0:T(8,128)(2,1)S(1)}, u32[]{:S(2)}, u32[]{:S(2)}) collective-permute-start(bf16[16,128,128]{2,1,0:T(8,128)(2,1)S(1)} %bitcast.38), channel_id=1, source_target_pairs={{0,1},{1,0},{2,3},{3,2},{4,5},{5,4},{6,7},{7,6},{8,9},{9,8},{10,11... | collective-permute-start | bytes 1572872 | tf_op jit(solution)/shard_map/ppermute | solution.py:23
  141.4 5.4 %collective-permute-start.1 = (bf16[256,128]{1,0:T(8,128)(2,1)S(1)}, bf16[256,128]{1,0:T(8,128)(2,1)S(1)}, u32[]{:S(2)}, u32[]{:S(2)}) collective-permute-start(bf16[256,128]{1,0:T(8,128)(2,1)S(1)} %bitcast.49), channel_id=1, source_target_pairs={{0,4},{4,8},{8,12},{1,5},{5,9},{9,13},{2,6},{6,10},{10,14},{3,7},{... | collective-permute-start | bytes 196616 | tf_op jit(solution)/shard_map/ppermute | solution.py:29
  143.9 4.8 %collective-permute-start.2 = (bf16[256,128]{1,0:T(8,128)(2,1)S(1)}, bf16[256,128]{1,0:T(8,128)(2,1)S(1)}, u32[]{:S(2)}, u32[]{:S(2)}) collective-permute-start(bf16[256,128]{1,0:T(8,128)(2,1)S(1)} %bitcast.50), channel_id=1, source_target_pairs={{0,4},{4,8},{8,12},{1,5},{5,9},{9,13},{2,6},{6,10},{10,14},{3,7},{... | collective-permute-start | bytes 196616 | tf_op jit(solution)/shard_map/ppermute | solution.py:29
Sparse Core Ops, SparseCore 0:
  34.1 70.6 reduce-scatter.4
  116.9 25.3 reduce-scatter.2
where the time goes:
time: 158 us; the launch traced here: 157 us
  waiting for transfers between devices  66.7 us (42%)
  blocking collectives  28.8 us (18%)
  starting transfers between devices  18 us (11%)
  matrix products  15.4 us (10%)
  between operations  13.6 us (9%)
  other arithmetic  11.2 us (7%)
  local copies, waits for them, and re-layouts  3.44 us (2%)
    reduce_scatter x2, waiting for transfers between devices, project_fold(): lax.psum_scatter(partial, ('mp', 'enc'), scatter_dimension=1, tiled=True)  42.8 us
    all_to_all x1, waiting for transfers between devices, local(): lax.all_to_all(packed, 'seq', split_axis=0, concat_axis=0, tiled=True)  20.9 us
    all_to_all x1, blocking collectives, project_fold(): lax.all_to_all(weight, ('mp', 'enc'), split_axis=0, concat_axis=1, tiled=...  18.7 us
    dot_general x2, matrix products, project_fold(): partial = jnp.dot(flat_rows, mine, preferred_element_type=jnp.float32)  11.3 us
    psum x1, blocking collectives, project_fold(): squares = lax.psum(jnp.sum(widened * widened, axis=1), ('mp', 'enc'))  10.1 us
    reduce_sum x2, other arithmetic, project_fold(): squares = lax.psum(jnp.sum(widened * widened, axis=1), ('mp', 'enc'))  5.83 us
    all_to_all x1, starting transfers between devices, local(): lax.all_to_all(sent_ids, 'seq', split_axis=0, concat_axis=0, tiled=True)  5.6 us
    all_to_all x1, starting transfers between devices, local(): lax.all_to_all(packed, 'seq', split_axis=0, concat_axis=0, tiled=True)  4.63 us
  transfers between devices with their start and end apart: 8, of which 4 were waited for; matrix products, arithmetic and copies ran while one was open for 12% of the time, Pallas kernels for 0%

commit v1 on v0

--- a/solution.py
+++ b/solution.py
@@ -11,6 +11,29 @@
 NB_SEQ = 16
 ENC_CAP = 24
 epsilon = 1e-05
+
+
+def cut_along(array, dim, peers):
+    shape = array.shape
+    blocks = array.reshape(*shape[:dim], peers, shape[dim] // peers, *shape[dim + 1 :])
+    return jnp.moveaxis(blocks, dim, 0)
+
+
+def laid_out(blocks, dim):
+    blocks = jnp.moveaxis(blocks, 0, dim)
+    shape = blocks.shape
+    return blocks.reshape(*shape[:dim], shape[dim] * shape[dim + 1], *shape[dim + 2 :])
+
+
+def exchange_in_pairs(array, axis, split_dim, concat_dim):
+    size, index = (lax.axis_size(axis), lax.axis_index(axis))
+    blocks = cut_along(array, split_dim, size)
+    outs = [blocks[index]]
+    for step in range(1, size):
+        sent = blocks[index ^ step]
+        outs.append(lax.ppermute(sent, axis, [(i, i ^ step) for i in range(size)]))
+    blocks = jnp.stack(outs)[index ^ jnp.arange(size)]
+    return laid_out(blocks, concat_dim)
 
 
 def partner_2(block, axis, stride):
@@ -88,7 +111,7 @@
     encoded = normalized(folded, 1.0).reshape(ENC_CAP, RLEN * head_size)
     packed = pack_rows(chosen, encoded, seq_count, pair_cap)
     received, received_ids = (
-        lax.all_to_all(packed, "seq", split_axis=0, concat_axis=0, tiled=True),
+        exchange_in_pairs(packed, "seq", 0, 0),
         lax.all_to_all(sent_ids, "seq", split_axis=0, concat_axis=0, tiled=True),
     )
     own_half = place_rows(received, received_ids).reshape(NB_SEQ, RLEN, head_size)

time: 158 us -> 149 us (0.943)
  waiting for transfers between devices: 66.7 us -> 40.1 us
  blocking collectives: 28.8 us -> 53.3 us
  starting transfers between devices: 18 us -> 12.8 us
    reduce_scatter x2, waiting for transfers between devices: 42.8 us -> 19.3 us  [project_fold(): lax.psum_scatter(partial, ('mp', 'enc'), scatter_dimension=1, tiled=True)]
    all_to_all x2 -> x0, waiting for transfers between devices: 20.9 us -> none  [the longest x1 20.9 us: local(): lax.all_to_all(packed, 'seq', split_axis=0, concat_axis=0, tiled=True)]
    ppermute x0 -> x3, waiting for transfers between devices: none -> 17.8 us  [exchange_in_pairs(): outs.append(lax.ppermute(sent, axis, [(i, i ^ step) for i in range(size)]))]
    psum x1, blocking collectives: 10.1 us -> 23.7 us  [project_fold(): squares = lax.psum(jnp.sum(widened * widened, axis=1), ('mp', 'enc'))]
    all_to_all x0 -> x1, blocking collectives: none -> 10.9 us  [local(): lax.all_to_all(sent_ids, 'seq', split_axis=0, concat_axis=0, tiled=True)]
    all_to_all x2 -> x0, starting transfers between devices: 10.2 us -> none  [the longest x1 5.6 us: local(): lax.all_to_all(sent_ids, 'seq', split_axis=0, concat_axis=0, tiled=True)]
    ppermute x0 -> x3, starting transfers between devices: none -> 4.45 us  [exchange_in_pairs(): outs.append(lax.ppermute(sent, axis, [(i, i ^ step) for i in range(size)]))]
  transfers between devices with their start and end apart: 8 -> 9, of which waited for: 4 -> 5; matrix products, arithmetic and copies ran while one was open for 12% -> 10% of each run, Pallas kernels for 0% -> 0%
where the time goes in v1:
time: 149 us; the launch traced here: 148 us
  blocking collectives  53.3 us (36%)
  waiting for transfers between devices  40.1 us (27%)
  matrix products  14.4 us (10%)
  between operations  13.7 us (9%)
  starting transfers between devices  12.8 us (9%)
  other arithmetic  9.83 us (7%)
  local copies, waits for them, and re-layouts  4.4 us (3%)
    psum x1, blocking collectives, project_fold(): squares = lax.psum(jnp.sum(widened * widened, axis=1), ('mp', 'enc'))  23.7 us
    reduce_scatter x2, waiting for transfers between devices, project_fold(): lax.psum_scatter(partial, ('mp', 'enc'), scatter_dimension=1, tiled=True)  19.3 us
    all_to_all x1, blocking collectives, project_fold(): lax.all_to_all(weight, ('mp', 'enc'), split_axis=0, concat_axis=1, tiled=...  18.7 us
    ppermute x3, waiting for transfers between devices, exchange_in_pairs(): outs.append(lax.ppermute(sent, axis, [(i, i ^ step) for i in range(size)]))  17.8 us
    dot_general x2, matrix products, project_fold(): partial = jnp.dot(flat_rows, mine, preferred_element_type=jnp.float32)  11.2 us
    all_to_all x1, blocking collectives, local(): lax.all_to_all(sent_ids, 'seq', split_axis=0, concat_axis=0, tiled=True)  10.9 us
    ppermute x2, starting transfers between devices, passed_along(): return lax.ppermute(block, axis, route)  4.67 us
    ppermute x3, starting transfers between devices, exchange_in_pairs(): outs.append(lax.ppermute(sent, axis, [(i, i ^ step) for i in range(size)]))  4.45 us
  transfers between devices with their start and end apart: 9, of which 5 were waited for; matrix products, arithmetic and copies ran while one was open for 10% of the time, Pallas kernels for 0%

profile of v1, /device:TPU:0, one launch (start us, length us, event | category | flops | bytes accessed | tf_op | source)
XLA Modules:
  0.0 148.5 jit_solution(10989234088725827523)
XLA Ops:
  6.5 18.7 %all_to_all.44 = bf16[4,1024,128]{2,1,0:T(8,128)(2,1)S(1)} all-to-all(bf16[4,1024,128]{2,1,0:T(8,128)(2,1)} %bitcast.54), channel_id=1, replica_groups=mesh['groups'=2,'seq'=4,'mp'=2,'enc'=2] {'mp','enc'}, dimensions={0} | all-to-all | bytes 2097152 | tf_op jit(solution)/shard_map/all_to_all | solution.py:58
  25.7 8.2 %fusion.34 = f32[3072,512]{1,0:T(8,128)} fusion(bf16[3072,1024]{1,0:T(8,128)(2,1)} %bitcast.48, bf16[1024,512]{0,1:T(8,128)(2,1)S(1)} %bitcast.56), kind=kOutput, calls=%fused_computation.62 | convolution fusion | flops 3221225472 | bytes 13631488 | tf_op jit(solution)/shard_map/dot_general | solution.py:59
  34.6 0.6 fusion.22
  35.3 0.6 iota_compare_fusion.4
  36.3 10.9 %all_to_all.45 = s32[4,1,8]{2,1,0:T(1,128)S(1)} all-to-all(s32[4,1,8]{2,1,0:T(1,128)S(1)} %bitcast.68), channel_id=1, replica_groups=mesh['groups'=2,'seq'=4,'mp'=2,'enc'=2] {'seq'}, dimensions={0} | all-to-all | bytes 256 | tf_op jit(solution)/shard_map/all_to_all | solution.py:115
  47.3 3.5 %all-to-all-start = ((bf16[4,1024,128]{2,1,0:T(8,128)(2,1)}), bf16[4,1024,128]{2,1,0:T(8,128)(2,1)S(1)}, u32[]{:S(2)}, u32[]{:S(2)}) async-start(bf16[4,1024,128]{2,1,0:T(8,128)(2,1)} %bitcast), calls=%async_computation | async-start | bytes 2097152 | tf_op jit(solution)/shard_map/all_to_all | solution.py:58
  50.9 4.1 %multiply_reduce_fusion = f32[24,128]{1,0:T(8,128)S(1)} fusion(bf16[24,128,1024]{2,1,0:T(8,128)(2,1)} %param.7), kind=kLoop, calls=%fused_computation.5 | loop fusion | flops 9434112 | bytes 6303744 | tf_op jit(solution)/shard_map/reduce_sum | solution.py:62
  55.2 23.7 %all-reduce = (f32[3072]{0:T(1024)S(1)}, f32[512]{0:T(512)S(1)}) all-reduce(f32[3072]{0:T(1024)S(1)} %bitcast.67, f32[512]{0:T(512)S(1)} %multiply_reduce_fusion.1), channel_id=1, replica_groups=mesh['groups'=2,'seq'=4,'mp'=2,'enc'=2] {'mp','enc'}, use_global_device_ids=true, to_apply=%region_8.9 | all-reduce | flops 3584 | bytes 28672 | tf_op jit(solution)/shard_map/psum | solution.py:62
  79.5 0.7 reduce.4
  80.2 1.4 copy.12
  81.6 19.3 %reduce-scatter.5.cloned.1.call-done = f32[3072,128]{1,0:T(8,128)} async-done(((f32[3072,512]{1,0:T(8,128)}), f32[3072,128]{1,0:T(8,128)}) %reduce-scatter.5.cloned.1.call-update) | async-done | bytes 1572880 | tf_op jit(solution)/shard_map/reduce_scatter | solution.py:60
  100.9 1.9 %multiply_convert_fusion = bf16[3072,128]{1,0:T(8,128)(2,1)S(1)} fusion(f32[3072,128]{1,0:T(8,128)} %reduce-scatter.5.cloned.1.call-done, f32[3072]{0:T(1024)S(1)} %add_rsqrt_fusion), kind=kLoop, calls=%fused_computation.7 | loop fusion | flops 786432 | bytes 2371584 | tf_op jit(solution)/shard_map/convert_element_type | solution.py:69
  103.8 0.7 collective-permute-start.2
  104.4 1.5 collective-permute-start.1
  105.9 2.3 %collective-permute-start = (bf16[1,8,16384]{2,1,0:T(8,128)(2,1)S(1)}, bf16[1,8,16384]{2,1,0:T(8,128)(2,1)S(1)}, u32[]{:S(2)}, u32[]{:S(2)}) collective-permute-start(bf16[1,8,16384]{2,1,0:T(8,128)(2,1)S(1)} %get-tuple-element.12), channel_id=1, source_target_pairs={{0,4},{4,0},{8,12},{12,8},{1,5},{5,1},{9,13},{13,9},{2,6},{6,2},{1... | collective-permute-start | bytes 786440 | tf_op jit(solution)/shard_map/ppermute | solution.py:34
  108.2 3.0 %fusion.33 = f32[512,512]{1,0:T(8,128)} fusion(bf16[512,1024]{1,0:T(8,128)(2,1)S(1)} %copy-done, bf16[1024,512]{0,1:T(8,128)(2,1)} %bitcast.55), kind=kOutput, calls=%fused_computation.61 | convolution fusion | flops 536870912 | bytes 3145728 | tf_op jit(solution)/shard_map/dot_general | solution.py:59
  111.2 3.7 %collective-permute-done.2 = bf16[1,8,16384]{2,1,0:T(8,128)(2,1)S(1)} collective-permute-done((bf16[1,8,16384]{2,1,0:T(8,128)(2,1)S(1)}, bf16[1,8,16384]{2,1,0:T(8,128)(2,1)S(1)}, u32[]{:S(2)}, u32[]{:S(2)}) %collective-permute-start.2) | collective-permute-done | bytes 262176 | tf_op jit(solution)/shard_map/ppermute | solution.py:34
  114.9 14.0 %collective-permute-done.1 = bf16[1,8,16384]{2,1,0:T(8,128)(2,1)S(1)} collective-permute-done((bf16[1,8,16384]{2,1,0:T(8,128)(2,1)S(1)}, bf16[1,8,16384]{2,1,0:T(8,128)(2,1)S(1)}, u32[]{:S(2)}, u32[]{:S(2)}) %collective-permute-start.1) | collective-permute-done | bytes 262176 | tf_op jit(solution)/shard_map/ppermute | solution.py:34
  130.2 1.9 %collective-permute-done.3 = bf16[16,128,128]{2,1,0:T(8,128)(2,1)S(1)} collective-permute-done((bf16[16,128,128]{2,1,0:T(8,128)(2,1)S(1)}, bf16[16,128,128]{2,1,0:T(8,128)(2,1)S(1)}, u32[]{:S(2)}, u32[]{:S(2)}) %collective-permute-start.3) | collective-permute-done | bytes 524320 | tf_op jit(solution)/shard_map/ppermute | solution.py:46
  132.2 1.3 collective-permute-start.4
  133.5 1.1 multiply_convert_fusion.1
  134.7 3.4 %collective-permute-start.5 = (bf16[256,128]{1,0:T(8,128)(2,1)S(1)}, bf16[256,128]{1,0:T(8,128)(2,1)S(1)}, u32[]{:S(2)}, u32[]{:S(2)}) collective-permute-start(bf16[256,128]{1,0:T(8,128)(2,1)S(1)} %bitcast.66), channel_id=1, source_target_pairs={{0,4},{4,8},{8,12},{1,5},{5,9},{9,13},{2,6},{6,10},{10,14},{3,7},{... | collective-permute-start | bytes 196616 | tf_op jit(solution)/shard_map/ppermute | solution.py:52
  138.9 1.1 collective-permute-done.5
  140.0 1.6 %convolution_convert_fusion.2 = bf16[8,64,128]{2,1,0:T(8,128)(2,1)} fusion(bf16[7,256,128]{2,1,0:T(8,128)(2,1)S(1)} %bitcast.59, bf16[1,256,128]{2,1,0:T(8,128)(2,1)S(1)} %bitcast.69, f32[8,64]{1,0:T(8,128)S(1)} %fusion.30, f32[8,64,256]{2,1,0:T(8,128)S(1)} %fusion.6), kind=kOutput, calls=%fused_computation.11 | convolution fusion | flops 34276096 | bytes 1181696 | tf_op jit(solution)/shard_map/cqk,ckd->cqd/dot_general | solution.py:129
  (43 shorter events, 5.6 us)
Async XLA Ops:
  6.5 94.4 %reduce-scatter.5.cloned.1.call-start = ((), (), s32[]{:S(2)}) async-start(), calls=%async_computation.6 | async-start | bytes 7864320 | tf_op jit(solution)/shard_map/reduce_scatter | solution.py:60
  34.0 0.7 copy-start.1
  34.0 1.9 %copy-start.2 = (s32[24]{0:T(128)S(1)}, s32[24]{0:T(128)}, u32[]{:S(2)}) copy-start(s32[24]{0:T(128)} %param.9) | copy-start | bytes 292
  34.0 21.0 %copy-start = (bf16[512,1024]{1,0:T(8,128)(2,1)S(1)}, bf16[512,1024]{1,0:T(8,128)(2,1)}, u32[]{:S(2)}) copy-start(bf16[512,1024]{1,0:T(8,128)(2,1)} %param.6) | copy-start | bytes 3145732
  47.3 33.0 %all-to-all-start = ((bf16[4,1024,128]{2,1,0:T(8,128)(2,1)}), bf16[4,1024,128]{2,1,0:T(8,128)(2,1)S(1)}, u32[]{:S(2)}, u32[]{:S(2)}) async-start(bf16[4,1024,128]{2,1,0:T(8,128)(2,1)} %bitcast), calls=%async_computation | async-start | bytes 2097152 | tf_op jit(solution)/shard_map/all_to_all | solution.py:58
  50.8 82.7 %reduce-scatter.3.cloned.1.call-start = ((), (), s32[]{:S(2)}) async-start(), calls=%async_computation.5 | async-start | bytes 1310720 | tf_op jit(solution)/shard_map/reduce_scatter | solution.py:60
  103.8 11.2 %collective-permute-start.2 = (bf16[1,8,16384]{2,1,0:T(8,128)(2,1)S(1)}, bf16[1,8,16384]{2,1,0:T(8,128)(2,1)S(1)}, u32[]{:S(2)}, u32[]{:S(2)}) collective-permute-start(bf16[1,8,16384]{2,1,0:T(8,128)(2,1)S(1)} %get-tuple-element.10), channel_id=1, source_target_pairs={{0,12},{4,8},{8,4},{12,0},{1,13},{5,9},{9,5},{13,1},{2,14},{6,10},... | collective-permute-start | bytes 786440 | tf_op jit(solution)/shard_map/ppermute | solution.py:34
  104.4 24.6 %collective-permute-start.1 = (bf16[1,8,16384]{2,1,0:T(8,128)(2,1)S(1)}, bf16[1,8,16384]{2,1,0:T(8,128)(2,1)S(1)}, u32[]{:S(2)}, u32[]{:S(2)}) collective-permute-start(bf16[1,8,16384]{2,1,0:T(8,128)(2,1)S(1)} %get-tuple-element.11), channel_id=1, source_target_pairs={{0,8},{4,12},{8,0},{12,4},{1,9},{5,13},{9,1},{13,5},{2,10},{6,14},... | collective-permute-start | bytes 786440 | tf_op jit(solution)/shard_map/ppermute | solution.py:34
  105.9 23.1 %collective-permute-start = (bf16[1,8,16384]{2,1,0:T(8,128)(2,1)S(1)}, bf16[1,8,16384]{2,1,0:T(8,128)(2,1)S(1)}, u32[]{:S(2)}, u32[]{:S(2)}) collective-permute-start(bf16[1,8,16384]{2,1,0:T(8,128)(2,1)S(1)} %get-tuple-element.12), channel_id=1, source_target_pairs={{0,4},{4,0},{8,12},{12,8},{1,5},{5,1},{9,13},{13,9},{2,6},{6,2},{1... | collective-permute-start | bytes 786440 | tf_op jit(solution)/shard_map/ppermute | solution.py:34
  130.1 2.0 %collective-permute-start.3 = (bf16[16,128,128]{2,1,0:T(8,128)(2,1)S(1)}, bf16[16,128,128]{2,1,0:T(8,128)(2,1)S(1)}, u32[]{:S(2)}, u32[]{:S(2)}) collective-permute-start(bf16[16,128,128]{2,1,0:T(8,128)(2,1)S(1)} %bitcast.51), channel_id=1, source_target_pairs={{0,1},{1,0},{2,3},{3,2},{4,5},{5,4},{6,7},{7,6},{8,9},{9,8},{10,11... | collective-permute-start | bytes 1572872 | tf_op jit(solution)/shard_map/ppermute | solution.py:46
  132.2 5.9 %collective-permute-start.4 = (bf16[256,128]{1,0:T(8,128)(2,1)S(1)}, bf16[256,128]{1,0:T(8,128)(2,1)S(1)}, u32[]{:S(2)}, u32[]{:S(2)}) collective-permute-start(bf16[256,128]{1,0:T(8,128)(2,1)S(1)} %bitcast.65), channel_id=1, source_target_pairs={{0,4},{4,8},{8,12},{1,5},{5,9},{9,13},{2,6},{6,10},{10,14},{3,7},{... | collective-permute-start | bytes 196616 | tf_op jit(solution)/shard_map/ppermute | solution.py:52
  134.7 5.3 %collective-permute-start.5 = (bf16[256,128]{1,0:T(8,128)(2,1)S(1)}, bf16[256,128]{1,0:T(8,128)(2,1)S(1)}, u32[]{:S(2)}, u32[]{:S(2)}) collective-permute-start(bf16[256,128]{1,0:T(8,128)(2,1)S(1)} %bitcast.66), channel_id=1, source_target_pairs={{0,4},{4,8},{8,12},{1,5},{5,9},{9,13},{2,6},{6,10},{10,14},{3,7},{... | collective-permute-start | bytes 196616 | tf_op jit(solution)/shard_map/ppermute | solution.py:52
Sparse Core Ops, SparseCore 0:
  34.1 66.7 reduce-scatter.4
  111.3 22.1 reduce-scatter.2
